TPU v7x, 256 devices: a whole 4x4x8 slice. The times are simulated.
256 devices in a mesh: section: 2 (over core), grp: 4 (over x), dev: 32 (over y, z).
Axes of the slice: x: 4, y: 4, z: 8, core: 2. Of those that a mesh axis runs over, the one named last changes fastest.
Arguments:
- frames: bfloat16 [4, 512, 512, 256], P('grp', 'dev', 'section'), may hold values from -6 to 6
- templates: bfloat16 [8192, 256], P('dev'), may hold values from -0.375 to 0.375
- pair_block: int32 [2, 4, 256], P('section', 'grp', 'dev'), may hold values from 0 to 63
- pair_tile: int32 [2, 4, 256], P('section', 'grp', 'dev'), may hold values from 0 to 3
- pair_count: int32 [2, 4, 32], P('section', 'grp', 'dev'), may hold values from 1 to 8, 128 in all within a row
- owner_order: int32 [8192], replicated, may hold values from 0 to 8191, each once
Outputs:
- quantities: float32 [4, 8192], P('grp', 'dev')
Inputs may be any that keep to these rules, and one draw needn't show every extreme that they name: `pair_count`: each device's count of live slots; the counts of one section half and run sum to half of all slots there, and one of them is 8. `owner_order`: A permutation of the precursors.
All inputs are finite; a program needn't handle non-finite values.
Results may differ from a plain program's by a relative error of at most 0.00037.
Values may be sent and summed in bfloat16 or wider, within the bound.
A program may use at most 64 MiB of HBM per device.

v0:
```python
import math
import jax
import jax.numpy as jnp
from jax import lax
from jax.sharding import PartitionSpec as P

MOB = 512
SCALES = 6
RAD = 4
TM = 64
PB = 128
PREC = 8192
retention_spread = 2.0


def extended(cells, sides, width):
    for axis, dim in sides:
        count = lax.axis_size(axis)
        ends = count - 1
        head = lax.slice_in_dim(cells, 0, width, axis=dim)
        tail = lax.slice_in_dim(cells, cells.shape[dim] - width, cells.shape[dim], axis=dim)
        cells = jnp.concatenate(
            [
                lax.ppermute(tail, axis, [(i, (i + 1) % count) for i in range(ends)]),
                cells,
                lax.ppermute(head, axis, [((i + 1) % count, i) for i in range(ends)]),
            ],
            axis=dim,
        )
    return cells


def retention_weights():
    bell_values = [
        math.exp(-0.5 * (offset / retention_spread) ** 2) for offset in range(-RAD, RAD + 1)
    ]
    bell_total = sum(bell_values)
    return [weight_value / bell_total for weight_value in bell_values]


def mobility_kernels(row_start, row_count):
    row_place = (row_start + jnp.arange(row_count, dtype=jnp.int32)).astype(jnp.float32)
    col_place = jnp.arange(MOB, dtype=jnp.int32).astype(jnp.float32)
    distance = row_place[:, None] - col_place[None, :]
    tables = []
    for level in range(SCALES):
        spread_scans = 2.0**level
        scaled = distance / spread_scans
        tables.append(
            (1.0 - scaled * scaled)
            * jnp.exp(-0.5 * scaled * scaled)
            / math.sqrt(0.75 * math.sqrt(math.pi) * spread_scans)
        )
    return jnp.stack(tables).astype(jnp.bfloat16)


def on_device(frames, templates, pair_block, pair_tile, pair_count, owner_order):
    section_index = lax.axis_index("section")
    weights = retention_weights()
    count_frames = frames.shape[1]
    mob_local = frames.shape[2]
    channels = frames.shape[3]
    framed = extended(frames, (("dev", 1),), RAD)
    padded = framed.astype(jnp.float32)
    smoothed = weights[0] * padded[:, 0:count_frames]
    for offset in range(1, 2 * RAD + 1):
        smoothed = smoothed + weights[offset] * padded[:, offset : offset + count_frames]
    smoothed = smoothed.astype(jnp.bfloat16)
    gathered = lax.all_gather(smoothed, "section", axis=2, tiled=True)
    kernels = mobility_kernels(section_index * mob_local, mob_local)
    wavelet_stack = jnp.einsum(
        "smn,fnc->smfc", kernels, gathered[0], preferred_element_type=jnp.float32
    ).astype(jnp.bfloat16)
    template_panel = lax.all_gather(templates, "dev", axis=0, tiled=True)
    blocks = template_panel.shape[0] // PB
    live_pairs = pair_count[0, 0, 0]
    block_ids = pair_block[0, 0]
    tile_ids = pair_tile[0, 0]

    def visit_pair(slot_index, totals):
        block_id = block_ids[slot_index]
        tile_id = tile_ids[slot_index]
        tile_cells = lax.dynamic_slice_in_dim(wavelet_stack, tile_id * TM, TM, 1).reshape(
            -1, channels
        )
        block_rows = lax.dynamic_slice_in_dim(template_panel, block_id * PB, PB, 0)
        scores = jnp.dot(tile_cells, block_rows.T, preferred_element_type=jnp.float32)
        response = jnp.mean(jnp.maximum(scores, 0.0), axis=0)
        block_hit = (jnp.arange(blocks, dtype=jnp.int32) == block_id).astype(jnp.float32)
        return totals + block_hit[:, None] * response[None, :]

    totals = lax.fori_loop(0, live_pairs, visit_pair, jnp.zeros((blocks, PB), jnp.float32))
    placed = jnp.zeros((PREC,), jnp.float32).at[owner_order].set(totals.reshape(-1))[None]
    summed = lax.psum(placed, "section")
    owned = lax.psum_scatter(summed, "dev", scatter_dimension=1, tiled=True)
    run_count = lax.axis_size("grp")
    run_mask = (jnp.arange(run_count, dtype=jnp.int32) == lax.axis_index("grp")).astype(jnp.float32)
    run_totals = lax.psum(run_mask * jnp.sum(owned), ("grp", "dev"))
    own_total = jnp.sum(run_totals * run_mask)
    factor = jnp.mean(run_totals) / own_total
    return owned * factor


def solution(mesh):
    placed = (
        P("grp", "dev", "section", None),
        P("dev", None),
        P("section", "grp", "dev"),
        P("section", "grp", "dev"),
        P("section", "grp", "dev"),
        P(),
    )
    return jax.shard_map(
        on_device, mesh=mesh, in_specs=placed, out_specs=P("grp", "dev"), check_vma=False
    )
```

profile of v0, /device:TPU:0, one launch (start us, length us, event | category | flops | bytes accessed | tf_op | source)
XLA Modules:
  0.0 833.9 jit_solution(16655650894832102042)
XLA Ops:
  6.5 1.3 fusion.63
  7.8 2.1 collective-permute-start
  9.9 1.3 collective-permute-start.1
  11.2 9.8 %collective-permute-done = bf16[1,4,256,256]{3,2,1,0:T(8,128)(2,1)S(1)} collective-permute-done((bf16[1,4,256,256]{3,2,1,0:T(8,128)(2,1)S(1)}, bf16[1,4,256,256]{3,2,1,0:T(8,128)(2,1)S(1)}, u32[]{:S(2)}, u32[]{:S(2)}) %collective-permute-start) | collective-permute-done | bytes 524320 | tf_op jit(solution)/shard_map/ppermute | solution.py:24
  21.1 4.3 collective-permute-done.1
  25.4 2.1 maximum_convert_fusion
  27.4 5.7 fusion.4
  33.2 0.7 all-gather.5.cloned.1.call-update
  34.3 0.3 fusion.54
  34.8 0.3 fusion.56
  35.0 0.3 fusion.57
  35.3 0.3 fusion.58
  35.6 19.7 %all-gather.3.cloned.1.call-done = bf16[1,16,512,256]{3,2,1,0:T(8,128)(2,1)} async-done(((bf16[1,16,256,256]{3,2,1,0:T(8,128)(2,1)}), bf16[1,16,512,256]{3,2,1,0:T(8,128)(2,1)}) %all-gather.3.cloned.1.call-update) | async-done | bytes 4194320 | tf_op jit(solution)/shard_map/all_gather | solution.py:69
  55.2 11.7 %convolution_convert_fusion = bf16[6,256,16,256]{3,1,2,0:T(8,128)(2,1)} fusion(bf16[1,16,512,256]{3,2,1,0:T(8,128)(2,1)} %all-gather.3.cloned.1.call-done, bf16[6,256,512]{2,1,0:T(8,128)(2,1)S(1)} %fusion.58), kind=kOutput, calls=%fused_computation.9 | convolution fusion | flops 6448742400 | bytes 18350080 | tf_op jit(solution)/shard_map/smn,fnc->smfc/dot_general | solution.py:71
  66.9 73.7 %all-gather.5.cloned.1.call-done = bf16[8192,256]{1,0:T(8,128)(2,1)} async-done(((bf16[256,256]{1,0:T(8,128)(2,1)}), bf16[8192,256]{1,0:T(8,128)(2,1)}) %all-gather.5.cloned.1.call-update) | async-done | bytes 4194320 | tf_op jit(solution)/shard_map/all_gather | solution.py:74
  140.7 10.7 %while.10 = (s32[]{:T(128)}, f32[64,128]{1,0:T(8,128)S(1)}, s32[]{:T(128)}, s32[8]{0:T(128)S(1)}, s32[8]{0:T(128)S(1)}, /*index=5*/bf16[6,256,16,256]{3,1,2,0:T(...) while((s32[]{:T(128)}, f32[64,128]{1,0:T(8,128)S(1)}, ...), condition=%wide.region_2.0_spmd, body=%wide.region_0.0_spmd.sunk | while | flops 404242560 | bytes 15862567 | solution.py:92
  141.4 0.6 dynamic_slice.21
  142.5 2.3 constant_dynamic-slice_fusion.2
  144.8 1.9 copy.14
  146.7 0.6 dynamic_slice.22
  147.9 2.2 fusion.70
  150.1 0.6 compare_convert_fusion.2
  151.4 30.5 %scatter_custom_fusion = f32[8192]{0:T(1024)S(1)} fusion(s32[8192]{0:T(1024)S(1)} %compare_select_fusion, f32[8192]{0:T(1024)S(1)} %bitcast.30, f32[]{:T(128)} %constant.32.clone.1), kind=kCustom, calls=%fused_computation.91 | custom fusion | bytes 32772 | tf_op jit(solution)/shard_map/scatter | solution.py:93
  181.9 2.6 copy.10
  184.6 288.7 %reduce-scatter.4.cloned.1.call-done = f32[256,1]{1,0:T(8,128)} async-done(((f32[8192,1]{1,0:T(8,128)}), f32[256,1]{1,0:T(8,128)}) %reduce-scatter.4.cloned.1.call-update) | async-done | bytes 1040
  473.2 1.0 copy.11
  474.2 2.5 psum.16
  476.7 0.6 reduce_sum.36
  477.3 0.6 compare_select_fusion.2
  477.9 346.8 %psum.15 = f32[4]{0:T(128)S(1)} all-reduce(f32[4]{0:T(128)S(1)} %compare_select_fusion.2), channel_id=1, replica_groups=mesh['section'=2,'grp'=4,'dev'=32] {'grp','dev'}, use_global_device_ids=true, to_apply=%region_7.0 | all-reduce | flops 4 | bytes 32 | tf_op jit(solution)/shard_map/psum | solution.py:98
  824.8 0.7 fusion.62
  826.8 0.6 broadcast_multiply_fusion.1
  (19 shorter events, 0.7 us)
Async XLA Ops:
  6.5 48.7 %all-gather.3.cloned.1.call-start = ((), (), s32[]{:S(2)}) async-start(), calls=%async_computation.1 | async-start | bytes 6291456 | tf_op jit(solution)/shard_map/all_gather | solution.py:69
  7.8 13.3 %collective-permute-start = (bf16[1,4,256,256]{3,2,1,0:T(8,128)(2,1)S(1)}, bf16[1,4,256,256]{3,2,1,0:T(8,128)(2,1)S(1)}, u32[]{:S(2)}, u32[]{:S(2)}) collective-permute-start(bf16[1,4,256,256]{3,2,1,0:T(8,128)(2,1)S(1)} %get-tuple-element.74), channel_id=1, source_target_pairs={{0,1},{1,2},{2,3},{3,4},{4,5},{5,6},{6,7},{7,8},{8,9},{9,10},{10,1... | collective-permute-start | bytes 1572872 | tf_op jit(solution)/shard_map/ppermute | solution.py:24
  9.9 15.4 %collective-permute-start.1 = (bf16[1,4,256,256]{3,2,1,0:T(8,128)(2,1)S(1)}, bf16[1,4,256,256]{3,2,1,0:T(8,128)(2,1)S(1)}, u32[]{:S(2)}, u32[]{:S(2)}) collective-permute-start(bf16[1,4,256,256]{3,2,1,0:T(8,128)(2,1)S(1)} %get-tuple-element.75), channel_id=1, source_target_pairs={{1,0},{2,1},{3,2},{4,3},{5,4},{6,5},{7,6},{8,7},{9,8},{10,9},{11,1... | collective-permute-start | bytes 1572872 | tf_op jit(solution)/shard_map/ppermute | solution.py:26
  27.4 6.6 copy-start
  33.2 107.5 %all-gather.5.cloned.1.call-start = ((), (), s32[]{:S(2)}) async-start(), calls=%async_computation.2 | async-start | bytes 4325376 | tf_op jit(solution)/shard_map/all_gather | solution.py:74
  33.9 439.3 %reduce-scatter.4.cloned.1.call-start = ((), (), s32[]{:S(2)}) async-start(), calls=%async_computation.3 | async-start | bytes 4325376
  35.5 105.1 %copy-start.1 = (s32[1,1,8]{2,1,0:T(1,128)S(1)}, s32[1,1,8]{2,1,0:T(1,128)}, u32[]{:S(2)}) copy-start(s32[1,1,8]{2,1,0:T(1,128)} %param.10) | copy-start | bytes 100
  35.6 105.1 %copy-start.2 = (s32[1,1,8]{2,1,0:T(1,128)S(1)}, s32[1,1,8]{2,1,0:T(1,128)}, u32[]{:S(2)}) copy-start(s32[1,1,8]{2,1,0:T(1,128)} %param.11) | copy-start | bytes 100
Sparse Core Ops, SparseCore 0:
  33.3 21.9 all-gather.2
  57.8 82.8 all-gather.4
  184.7 288.5 reduce-scatter.3
where the time goes:
time: 835 us; the launch traced here: 834 us
  waiting for transfers between devices  397 us (48%)
  blocking collectives  349 us (42%)
  local copies, waits for them, and re-layouts  40.7 us (5%)
  between operations  14.6 us (2%)
  matrix products  13.9 us (2%)
  other arithmetic  12.4 us (1%)
    psum x1, blocking collectives, on_device(): run_totals = lax.psum(run_mask * jnp.sum(owned), ('grp', 'dev'))  347 us
    unnamed x4, waiting for transfers between devices  289 us
    all_gather x1, waiting for transfers between devices, on_device(): template_panel = lax.all_gather(templates, 'dev', axis=0, tiled=True)  73.7 us
    scatter x1, local copies, waits for them, and re-layouts, on_device(): jnp.zeros((PREC,), jnp.float32).at[owner_order].set(totals.reshape(-1))  30.5 us
    all_gather x1, waiting for transfers between devices, on_device(): gathered = lax.all_gather(smoothed, 'section', axis=2, tiled=True)  19.7 us
  transfers between devices with their start and end apart: 5, of which 5 were waited for; matrix products, arithmetic and copies ran while one was open for 2% of the time, Pallas kernels for 0%

commit v1 on v0

--- a/solution.py
+++ b/solution.py
@@ -95,7 +95,9 @@
     owned = lax.psum_scatter(summed, "dev", scatter_dimension=1, tiled=True)
     run_count = lax.axis_size("grp")
     run_mask = (jnp.arange(run_count, dtype=jnp.int32) == lax.axis_index("grp")).astype(jnp.float32)
-    run_totals = lax.psum(run_mask * jnp.sum(owned), ("grp", "dev"))
+    run_totals = run_mask * jnp.sum(owned)
+    for j0 in ("dev", "grp"):
+        run_totals = lax.psum(run_totals, j0)
     own_total = jnp.sum(run_totals * run_mask)
     factor = jnp.mean(run_totals) / own_total
     return owned * factor

time: 835 us -> 571 us (0.68)
  blocking collectives: 349 us -> 85.1 us
    psum x1 -> x2, blocking collectives: 347 us -> 82.6 us  [on_device(): run_totals = lax.psum(run_totals, j0)]
where the time goes in v1:
time: 571 us; the launch traced here: 570 us
  waiting for transfers between devices  397 us (70%)
  blocking collectives  85.1 us (15%)
  local copies, waits for them, and re-layouts  40.7 us (7%)
  between operations  14.6 us (3%)
  matrix products  13.9 us (2%)
  other arithmetic  12.4 us (2%)
    unnamed x4, waiting for transfers between devices  289 us
    psum x2, blocking collectives, on_device(): run_totals = lax.psum(run_totals, j0)  82.6 us
    all_gather x1, waiting for transfers between devices, on_device(): template_panel = lax.all_gather(templates, 'dev', axis=0, tiled=True)  73.7 us
    scatter x1, local copies, waits for them, and re-layouts, on_device(): jnp.zeros((PREC,), jnp.float32).at[owner_order].set(totals.reshape(-1))  30.5 us
    all_gather x1, waiting for transfers between devices, on_device(): gathered = lax.all_gather(smoothed, 'section', axis=2, tiled=True)  19.7 us
    dot_general x1, matrix products, on_device(): jnp.einsum('smn,fnc->smfc', kernels, gathered[0], preferred_element_type=...  11.7 us
  transfers between devices with their start and end apart: 5, of which 5 were waited for; matrix products, arithmetic and copies ran while one was open for 2% of the time, Pallas kernels for 0%

profile of v1, /device:TPU:0, one launch (start us, length us, event | category | flops | bytes accessed | tf_op | source)
XLA Modules:
  0.0 569.7 jit_solution(9671011822080812713)
XLA Ops:
  6.5 1.3 fusion.63
  7.8 2.1 collective-permute-start
  9.9 1.3 collective-permute-start.1
  11.2 9.8 %collective-permute-done = bf16[1,4,256,256]{3,2,1,0:T(8,128)(2,1)S(1)} collective-permute-done((bf16[1,4,256,256]{3,2,1,0:T(8,128)(2,1)S(1)}, bf16[1,4,256,256]{3,2,1,0:T(8,128)(2,1)S(1)}, u32[]{:S(2)}, u32[]{:S(2)}) %collective-permute-start) | collective-permute-done | bytes 524320 | tf_op jit(solution)/shard_map/ppermute | solution.py:24
  21.1 4.3 collective-permute-done.1
  25.4 2.1 maximum_convert_fusion
  27.4 5.7 %fusion.4 = bf16[1,16,256,256]{3,2,1,0:T(8,128)(2,1)} fusion(f32[1,24,256,256]{3,2,1,0:T(8,128)S(1)} %maximum_convert_fusion), kind=kLoop, calls=%fused_computation.12 | loop fusion | flops 18874368 | bytes 39845888 | tf_op jit(solution)/shard_map/convert_element_type | solution.py:68
  33.2 0.7 all-gather.5.cloned.1.call-update
  34.8 0.3 fusion.56
  35.0 0.3 fusion.57
  35.3 0.3 fusion.58
  35.6 19.7 %all-gather.3.cloned.1.call-done = bf16[1,16,512,256]{3,2,1,0:T(8,128)(2,1)} async-done(((bf16[1,16,256,256]{3,2,1,0:T(8,128)(2,1)}), bf16[1,16,512,256]{3,2,1,0:T(8,128)(2,1)}) %all-gather.3.cloned.1.call-update) | async-done | bytes 4194320 | tf_op jit(solution)/shard_map/all_gather | solution.py:69
  55.2 11.7 %convolution_convert_fusion = bf16[6,256,16,256]{3,1,2,0:T(8,128)(2,1)} fusion(bf16[1,16,512,256]{3,2,1,0:T(8,128)(2,1)} %all-gather.3.cloned.1.call-done, bf16[6,256,512]{2,1,0:T(8,128)(2,1)S(1)} %fusion.58), kind=kOutput, calls=%fused_computation.9 | convolution fusion | flops 6448742400 | bytes 18350080 | tf_op jit(solution)/shard_map/smn,fnc->smfc/dot_general | solution.py:71
  66.9 73.7 %all-gather.5.cloned.1.call-done = bf16[8192,256]{1,0:T(8,128)(2,1)} async-done(((bf16[256,256]{1,0:T(8,128)(2,1)}), bf16[8192,256]{1,0:T(8,128)(2,1)}) %all-gather.5.cloned.1.call-update) | async-done | bytes 4194320 | tf_op jit(solution)/shard_map/all_gather | solution.py:74
  140.7 10.7 %while.10 = (s32[]{:T(128)}, f32[64,128]{1,0:T(8,128)S(1)}, s32[]{:T(128)}, s32[8]{0:T(128)S(1)}, s32[8]{0:T(128)S(1)}, /*index=5*/bf16[6,256,16,256]{3,1,2,0:T(...) while((s32[]{:T(128)}, f32[64,128]{1,0:T(8,128)S(1)}, ...), condition=%wide.region_2.0_spmd, body=%wide.region_0.0_spmd.sunk | while | flops 404242560 | bytes 15862567 | solution.py:92
  141.4 0.6 dynamic_slice.21
  142.5 2.3 constant_dynamic-slice_fusion.2
  144.8 1.9 copy.14
  146.7 0.6 dynamic_slice.22
  147.9 2.2 fusion.70
  150.1 0.6 compare_convert_fusion.2
  151.4 30.5 %scatter_custom_fusion = f32[8192]{0:T(1024)S(1)} fusion(s32[8192]{0:T(1024)S(1)} %compare_select_fusion, f32[8192]{0:T(1024)S(1)} %bitcast.30, f32[]{:T(128)} %constant.32.clone.1), kind=kCustom, calls=%fused_computation.91 | custom fusion | bytes 32772 | tf_op jit(solution)/shard_map/scatter | solution.py:93
  181.9 2.6 copy.10
  184.6 288.7 %reduce-scatter.4.cloned.1.call-done = f32[256,1]{1,0:T(8,128)} async-done(((f32[8192,1]{1,0:T(8,128)}), f32[256,1]{1,0:T(8,128)}) %reduce-scatter.4.cloned.1.call-update) | async-done | bytes 1040
  473.2 1.0 copy.11
  474.2 2.5 psum.24
  476.7 0.6 reduce_sum.36
  477.3 0.6 compare_select_fusion.2
  477.9 72.2 %psum.22 = f32[4]{0:T(128)S(1)} all-reduce(f32[4]{0:T(128)S(1)} %compare_select_fusion.2), channel_id=1, replica_groups=mesh['section'=2,'grp'=4,'dev'=32] {'dev'}, use_global_device_ids=true, to_apply=%region_7.0 | all-reduce | flops 4 | bytes 32 | tf_op jit(solution)/shard_map/psum | solution.py:100
  550.1 10.4 %psum.23 = f32[4]{0:T(128)S(1)} all-reduce(f32[4]{0:T(128)S(1)} %psum.22), channel_id=1, replica_groups=mesh['section'=2,'grp'=4,'dev'=32] {'grp'}, use_global_device_ids=true, to_apply=%region_8.0 | all-reduce | flops 4 | bytes 32 | tf_op jit(solution)/shard_map/psum | solution.py:100
  560.5 0.7 fusion.62
  562.6 0.6 broadcast_multiply_fusion.1
  (20 shorter events, 1.0 us)
Async XLA Ops:
  6.5 48.7 %all-gather.3.cloned.1.call-start = ((), (), s32[]{:S(2)}) async-start(), calls=%async_computation.1 | async-start | bytes 6291456 | tf_op jit(solution)/shard_map/all_gather | solution.py:69
  7.8 13.3 %collective-permute-start = (bf16[1,4,256,256]{3,2,1,0:T(8,128)(2,1)S(1)}, bf16[1,4,256,256]{3,2,1,0:T(8,128)(2,1)S(1)}, u32[]{:S(2)}, u32[]{:S(2)}) collective-permute-start(bf16[1,4,256,256]{3,2,1,0:T(8,128)(2,1)S(1)} %get-tuple-element.74), channel_id=1, source_target_pairs={{0,1},{1,2},{2,3},{3,4},{4,5},{5,6},{6,7},{7,8},{8,9},{9,10},{10,1... | collective-permute-start | bytes 1572872 | tf_op jit(solution)/shard_map/ppermute | solution.py:24
  9.9 15.4 %collective-permute-start.1 = (bf16[1,4,256,256]{3,2,1,0:T(8,128)(2,1)S(1)}, bf16[1,4,256,256]{3,2,1,0:T(8,128)(2,1)S(1)}, u32[]{:S(2)}, u32[]{:S(2)}) collective-permute-start(bf16[1,4,256,256]{3,2,1,0:T(8,128)(2,1)S(1)} %get-tuple-element.75), channel_id=1, source_target_pairs={{1,0},{2,1},{3,2},{4,3},{5,4},{6,5},{7,6},{8,7},{9,8},{10,9},{11,1... | collective-permute-start | bytes 1572872 | tf_op jit(solution)/shard_map/ppermute | solution.py:26
  27.4 6.6 %copy-start = (s32[8192]{0:T(1024)S(1)}, s32[8192]{0:T(1024)}, u32[]{:S(2)}) copy-start(s32[8192]{0:T(1024)} %param.13) | copy-start | bytes 98308
  33.2 107.5 %all-gather.5.cloned.1.call-start = ((), (), s32[]{:S(2)}) async-start(), calls=%async_computation.2 | async-start | bytes 4325376 | tf_op jit(solution)/shard_map/all_gather | solution.py:74
  33.9 439.3 %reduce-scatter.4.cloned.1.call-start = ((), (), s32[]{:S(2)}) async-start(), calls=%async_computation.3 | async-start | bytes 4325376
  35.5 105.1 %copy-start.1 = (s32[1,1,8]{2,1,0:T(1,128)S(1)}, s32[1,1,8]{2,1,0:T(1,128)}, u32[]{:S(2)}) copy-start(s32[1,1,8]{2,1,0:T(1,128)} %param.10) | copy-start | bytes 100
  35.6 105.1 %copy-start.2 = (s32[1,1,8]{2,1,0:T(1,128)S(1)}, s32[1,1,8]{2,1,0:T(1,128)}, u32[]{:S(2)}) copy-start(s32[1,1,8]{2,1,0:T(1,128)} %param.11) | copy-start | bytes 100
Sparse Core Ops, SparseCore 0:
  33.3 21.9 all-gather.2
  57.8 82.8 all-gather.4
  184.7 288.5 reduce-scatter.3
